TPU v7x, 256 devices: a whole 4x4x8 slice. The times are simulated.
256 devices in a mesh: rows: 64 (over z, y, core), cols: 4 (over x).
Axes of the slice: x: 4, y: 4, z: 8, core: 2. Of those that a mesh axis runs over, the one named last changes fastest.
Arguments:
- snapshot: float32 [24576, 8192], P('rows', 'cols'), may hold values from -270 to 270
- test_matrix: float32 [8192, 256], P('cols'), may hold values from -0.0625 to 0.0625
Outputs:
- projected: float32 [8192, 256], P('cols')
- triangle: float32 [256, 256], replicated
All inputs are finite; a program needn't handle non-finite values.
Results may differ from a plain program's by a relative error of at most 0.00007.
Values sent between devices are 32-bit elements; how exact they have to be, the bound alone decides.
A program may use at most 64 MiB of HBM per device.

v0:
```python
import jax
import jax.numpy as jnp
from jax import lax
from jax.sharding import Mesh
from jax.sharding import PartitionSpec as P

ROWS = ("rows_0", "rows_1", "rows_2")


high = lax.Precision.HIGHEST


def copy_for_each(array, axis):
    copies = jnp.broadcast_to(array, (lax.axis_size(axis), *array.shape))
    return lax.all_to_all(copies, axis, split_axis=0, concat_axis=0, tiled=True)


def taken_together(array, axis):
    everything = copy_for_each(array, axis)
    return jnp.sum(everything, axis=0)


def cut_along(array, dim, size):
    shape = array.shape
    blocks = array.reshape(*shape[:dim], size, shape[dim] // size, *shape[dim + 1 :])
    return jnp.moveaxis(blocks, dim, 0)


def summed_on_arrival(array, axis, dim):
    blocks = cut_along(array, dim, lax.axis_size(axis))
    arrived = lax.all_to_all(blocks, axis, split_axis=0, concat_axis=0, tiled=True)
    return arrived.sum(axis=0)


def summed_rows(array, axes, dim):
    far, near = axes
    blocks = cut_along(array, dim, lax.axis_size(far))
    nearer = summed_on_arrival(blocks, near, dim + 1)
    arrived = lax.all_to_all(nearer, far, split_axis=0, concat_axis=0, tiled=True)
    return arrived.sum(axis=0)


def padded_to(lines, size):
    spare = -len(lines) % size
    return jnp.pad(lines, [(0, spare)] + [(0, 0)] * (lines.ndim - 1))


def laid_out(blocks, dim):
    blocks = jnp.moveaxis(blocks, 0, dim)
    shape = blocks.shape
    return blocks.reshape(*shape[:dim], shape[dim] * shape[dim + 1], *shape[dim + 2 :])


def whole_of(array, axes, dim):
    far, near = axes
    blocks = copy_for_each(copy_for_each(array, far), near)
    return laid_out(blocks.swapaxes(0, 1).reshape(-1, *array.shape), dim)


def total_of(array, axes):
    lines = array.reshape(-1, array.shape[-1])
    own = summed_rows(padded_to(lines, lax.axis_size(axes[0]) * lax.axis_size(axes[1])), axes, 0)
    whole = whole_of(own, axes, 0)
    return whole[: len(lines)].reshape(array.shape)


def inner(left, right):
    return jnp.dot(left.T, right, precision=high, preferred_element_type=jnp.float32)


def body(snapshot, test_matrix):
    partial_sketch = jnp.dot(
        snapshot, test_matrix, precision=high, preferred_element_type=jnp.float32
    )
    sketch = taken_together(partial_sketch, "cols")
    local_gram = inner(sketch, sketch)
    gram = total_of(local_gram, (("rows_0", "rows_1"), "rows_2"))
    lower = jnp.linalg.cholesky(gram)
    basis = jax.scipy.linalg.solve_triangular(lower, sketch.T, lower=True).T
    projected = total_of(inner(snapshot, basis), (("rows_0", "rows_1"), "rows_2"))
    total = snapshot.shape[0] * lax.axis_size(ROWS)
    triangle = lower.T / jnp.sqrt(jnp.float32(total))
    return (projected, triangle)


def solution(mesh):
    finer = Mesh(
        mesh.devices.reshape(8, 4, 2, mesh.shape["cols"]), ("rows_0", "rows_1", "rows_2", "cols")
    )
    return jax.shard_map(
        body,
        mesh=finer,
        in_specs=(P(ROWS, "cols"), P("cols", None)),
        out_specs=(P("cols", None), P()),
        check_vma=False,
    )
```

profile of v0, /device:TPU:1, one launch (start us, length us, event | category | flops | bytes accessed | tf_op | source)
XLA Modules:
  0.0 273.3 jit_solution(17304677989599364028)
XLA Ops:
  0.6 1.9 copy-done
  2.5 4.2 %fusion.16 = f32[384,256]{1,0:T(8,128)S(1)} fusion(f32[384,2048]{1,0:T(8,128)S(1)} %copy-done, f32[2048,256]{1,0:T(8,128)} %param.3), kind=kOutput, calls=%fused_computation.38 | convolution fusion | flops 2415919104 | bytes 5636096 | tf_op jit(solution)/shard_map/dot_general | solution.py:72
  6.9 23.8 %all_to_all.45 = f32[4,384,256]{2,1,0:T(8,128)} all-to-all(f32[4,384,256]{2,1,0:T(8,128)S(1)} %broadcast_in_dim.17), channel_id=1, replica_groups=mesh['rows_0'=8,'rows_1'=4,'rows_2'=2,'cols'=4] {'cols'}, dimensions={0} | all-to-all | bytes 3145728 | tf_op jit(solution)/shard_map/all_to_all | solution.py:15
  30.7 2.3 reduce_sum.45
  35.0 1.7 convolution_bitcast_fusion.1
  36.8 6.9 %all_to_all.46 = f32[2,32,4,256]{3,1,2,0:T(8,128)} all-to-all(f32[2,32,4,256]{3,1,2,0:T(8,128)S(1)} %convolution_bitcast_fusion.1), channel_id=1, replica_groups=mesh['rows_0'=8,'rows_1'=4,'rows_2'=2,'cols'=4] {'rows_2'}, dimensions={0} | all-to-all | bytes 524288 | tf_op jit(solution)/shard_map/all_to_all | solution.py:31
  43.6 1.6 reduce_sum.46
  46.3 20.5 %all_to_all.47 = f32[32,4,256]{2,1,0:T(4,128)} all-to-all(f32[32,4,256]{2,1,0:T(4,128)S(1)} %copy.37), channel_id=1, replica_groups=mesh['rows_0'=8,'rows_1'=4,'rows_2'=2,'cols'=4] {'rows_0','rows_1'}, dimensions={0} | all-to-all | bytes 262144 | tf_op jit(solution)/shard_map/all_to_all | solution.py:39
  68.4 4.6 %all-to-all-start.3 = ((f32[32,4,256]{2,1,0:T(4,128)}), f32[32,4,256]{2,1,0:T(4,128)}, u32[]{:S(2)}, u32[]{:S(2)}) async-start(f32[32,4,256]{2,1,0:T(4,128)} %broadcast_in_dim.18), calls=%async_computation.3 | async-start | bytes 262144 | tf_op jit(solution)/shard_map/all_to_all | solution.py:15
  73.0 9.4 %all-to-all-done.3 = f32[32,4,256]{2,1,0:T(4,128)} async-done(((f32[32,4,256]{2,1,0:T(4,128)}), f32[32,4,256]{2,1,0:T(4,128)}, u32[]{:S(2)}, u32[]{:S(2)}) %all-to-all-start.3) | async-done | bytes 131104 | tf_op jit(solution)/shard_map/all_to_all | solution.py:15
  83.3 6.9 %all_to_all.48 = f32[2,32,4,256]{3,2,1,0:T(4,128)S(1)} all-to-all(f32[2,32,4,256]{3,2,1,0:T(4,128)S(1)} %broadcast_in_dim.19), channel_id=1, replica_groups=mesh['rows_0'=8,'rows_1'=4,'rows_2'=2,'cols'=4] {'rows_2'}, dimensions={0} | all-to-all | bytes 524288 | tf_op jit(solution)/shard_map/all_to_all | solution.py:15
  90.9 1.7 reshape_reshape.10
  92.6 1.8 copy.39
  96.8 13.2 %cholesky.50 = f32[128,128]{1,0:T(8,128)} custom-call(f32[128,128]{1,0:T(8,128)} %cholesky.118), custom_call_target="Cholesky" | custom-call | tf_op jit(solution)/shard_map/jit(cholesky)/cholesky | solution.py:78
  113.0 11.3 %custom-call.15 = f32[1,128,128]{1,2,0:T(8,128)} custom-call(f32[1,128,128]{2,1,0:T(8,128)} %get-tuple-element.37), custom_call_target="InvertDiagBlocksLowerTriangular" | custom-call | tf_op jit(solution)/shard_map/jit(cholesky)/cholesky | solution.py:78
  124.3 1.7 constant_dynamic-update-slice_fusion.1
  126.0 1.7 convolution_subtract_fusion.1
  127.7 13.2 %cholesky.105 = f32[128,128]{1,0:T(8,128)} custom-call(f32[128,128]{1,0:T(8,128)} %convolution_subtract_fusion.1), custom_call_target="Cholesky" | custom-call | tf_op jit(solution)/shard_map/jit(cholesky)/cholesky | solution.py:78
  144.2 1.8 multiply_bitcast_fusion
  146.1 6.8 %while.1 = (s32[]{:T(128)}, f32[256,256]{1,0:T(8,128)}, s32[2,2]{1,0:T(2,128)S(1)}, f32[2,128,128]{2,1,0:T(8,128)}, s32[]{:T(128)}) while((s32[]{:T(128)}, f32[256,256]{1,0:T(8,128)}, s32[2,2]{1,0:T(2,128)S(1)}, f32[2,128,128]{2,1,0:T(8,128)}, s32[]{:T(128)}) %tuple.34), condition=%wide.while_cond, body=%wide.while_body.sunk | while | flops 2 | bytes 132205 | solution.py:79
  146.7 2.9 %bitcast_dynamic-update-slice_fusion.2 = f32[2,128,128]{2,1,0:T(8,128)} fusion(f32[2,128,128]{2,1,0:T(8,128)} %get-tuple-element.79, s32[]{:T(128)S(6)} %copy.52, f32[256,256]{1,0:T(8,128)} %get-tuple-element.82, s32[]{:T(128)} %bitcast.51, s32[]{:T(128)} %bitcast.52), kind=kLoop, calls=%fused_computation.clone.1 | loop fusion | bytes 132100 | tf_op jit(solution)/shard_map/jit(_solve_triangular)/triangular_solve
  150.1 2.8 %bitcast_dynamic-update-slice_fusion.2 = f32[2,128,128]{2,1,0:T(8,128)} fusion(f32[2,128,128]{2,1,0:T(8,128)} %get-tuple-element.79, s32[]{:T(128)S(6)} %copy.52, f32[256,256]{1,0:T(8,128)} %get-tuple-element.82, s32[]{:T(128)} %bitcast.51, s32[]{:T(128)} %bitcast.52), kind=kLoop, calls=%fused_computation.clone.1 | loop fusion | bytes 132100 | tf_op jit(solution)/shard_map/jit(_solve_triangular)/triangular_solve
  152.9 21.1 %custom-call.16 = f32[2,128,128]{1,2,0:T(8,128)} custom-call(f32[2,128,128]{2,1,0:T(8,128)} %get-tuple-element.9), custom_call_target="InvertDiagBlocksLowerTriangular" | custom-call | tf_op jit(solution)/shard_map/jit(_solve_triangular)/triangular_solve | solution.py:79
  177.6 4.9 %convolution_bitcast_fusion = f32[2048,256]{0,1:T(8,128)} fusion(f32[384,2048]{1,0:T(8,128)S(1)} %copy-done, f32[128,384]{1,0:T(8,128)S(1)} %fusion.10, f32[128,384]{1,0:T(8,128)S(1)} %fusion.7), kind=kOutput, calls=%fused_computation.2 | convolution fusion | flops 2416017408 | bytes 5636096 | tf_op jit(solution)/shard_map/dot_general | solution.py:68
  182.5 2.9 %copy.40 = f32[2048,256]{1,0:T(8,128)} copy(f32[2048,256]{0,1:T(8,128)} %convolution_bitcast_fusion) | data formatting | bytes 4194304 | tf_op jit(solution)/shard_map/dot_general | solution.py:68
  185.4 1.7 copy.41
  187.2 6.3 %all_to_all.49 = f32[2,32,32,256]{3,2,1,0:T(8,128)} all-to-all(f32[2,32,32,256]{3,2,1,0:T(8,128)S(1)} %copy.41), channel_id=1, replica_groups=mesh['rows_0'=8,'rows_1'=4,'rows_2'=2,'cols'=4] {'rows_2'}, dimensions={0} | all-to-all | bytes 4194304 | tf_op jit(solution)/shard_map/all_to_all | solution.py:31
  193.4 2.8 %reduce_sum.48 = f32[32,32,256]{2,1,0:T(8,128)} reduce(f32[2,32,32,256]{3,2,1,0:T(8,128)} %all_to_all.49, f32[]{:T(128)} %constant.78.clone.1), dimensions={0}, to_apply=%region_7.8 | reduce | flops 262144 | bytes 3145732 | tf_op jit(solution)/shard_map/reduce_sum | solution.py:32
  196.3 31.9 %all_to_all.50 = f32[32,32,256]{2,1,0:T(8,128)} all-to-all(f32[32,32,256]{2,1,0:T(8,128)} %reduce_sum.48), channel_id=1, replica_groups=mesh['rows_0'=8,'rows_1'=4,'rows_2'=2,'cols'=4] {'rows_0','rows_1'}, dimensions={0} | all-to-all | bytes 2097152 | tf_op jit(solution)/shard_map/all_to_all | solution.py:39
  230.5 5.8 %all-to-all-start.7 = ((f32[32,32,256]{2,1,0:T(8,128)}), f32[32,32,256]{2,1,0:T(8,128)}, u32[]{:S(2)}, u32[]{:S(2)}) async-start(f32[32,32,256]{2,1,0:T(8,128)} %broadcast_in_dim.20), calls=%async_computation.7 | async-start | bytes 2097152 | tf_op jit(solution)/shard_map/all_to_all | solution.py:15
  237.2 24.8 %all-to-all-done.7 = f32[32,32,256]{2,1,0:T(8,128)} async-done(((f32[32,32,256]{2,1,0:T(8,128)}), f32[32,32,256]{2,1,0:T(8,128)}, u32[]{:S(2)}, u32[]{:S(2)}) %all-to-all-start.7) | async-done | bytes 1048608 | tf_op jit(solution)/shard_map/all_to_all | solution.py:15
  263.5 8.4 %all_to_all.51 = f32[2,32,32,256]{3,2,1,0:T(8,128)S(1)} all-to-all(f32[2,32,32,256]{3,2,1,0:T(8,128)S(1)} %broadcast_in_dim.21), channel_id=1, replica_groups=mesh['rows_0'=8,'rows_1'=4,'rows_2'=2,'cols'=4] {'rows_2'}, dimensions={0} | all-to-all | bytes 4194304 | tf_op jit(solution)/shard_map/all_to_all | solution.py:15
  (34 shorter events, 25.0 us)
Async XLA Ops:
  0.6 1.9 copy-start
  68.4 14.0 %all-to-all-start.3 = ((f32[32,4,256]{2,1,0:T(4,128)}), f32[32,4,256]{2,1,0:T(4,128)}, u32[]{:S(2)}, u32[]{:S(2)}) async-start(f32[32,4,256]{2,1,0:T(4,128)} %broadcast_in_dim.18), calls=%async_computation.3 | async-start | bytes 262144 | tf_op jit(solution)/shard_map/all_to_all | solution.py:15
  95.5 0.7 copy-start.2
  228.1 8.3 %copy-start.1 = (f32[256,256]{0,1:T(8,128)S(1)}, f32[256,256]{0,1:T(8,128)}, u32[]{:S(2)}) copy-start(f32[256,256]{0,1:T(8,128)} %get-tuple-element.32) | copy-start | bytes 786436
  230.5 31.4 %all-to-all-start.7 = ((f32[32,32,256]{2,1,0:T(8,128)}), f32[32,32,256]{2,1,0:T(8,128)}, u32[]{:S(2)}, u32[]{:S(2)}) async-start(f32[32,32,256]{2,1,0:T(8,128)} %broadcast_in_dim.20), calls=%async_computation.7 | async-start | bytes 2097152 | tf_op jit(solution)/shard_map/all_to_all | solution.py:15
where the time goes:
time: 275 us; the launch traced here: 273 us
  blocking collectives  105 us (38%)
  other arithmetic  74.2 us (27%)
  waiting for transfers between devices  34.1 us (12%)
  local copies, waits for them, and re-layouts  30.2 us (11%)
  matrix products  17.8 us (6%)
  starting transfers between devices  10.4 us (4%)
    all_to_all x2, blocking collectives, summed_rows(): lax.all_to_all(nearer, far, split_axis=0, concat_axis=0, tiled=True)  52.3 us
    another operation x6, other arithmetic, body(): lower = jnp.linalg.cholesky(gram)  41.2 us
    all_to_all x3, blocking collectives, copy_for_each(): return lax.all_to_all(copies, axis, split_axis=0, concat_axis=0, tiled=True)  39.2 us
    all_to_all x2, waiting for transfers between devices, copy_for_each(): return lax.all_to_all(copies, axis, split_axis=0, concat_axis=0, tiled=True)  34.1 us
    another operation x2, other arithmetic, body(): basis = jax.scipy.linalg.solve_triangular(lower, sketch.T, lower=True).T  21.1 us
    all_to_all x2, blocking collectives, summed_on_arrival(): lax.all_to_all(blocks, axis, split_axis=0, concat_axis=0, tiled=True)  13.1 us
    all_to_all x2, starting transfers between devices, copy_for_each(): return lax.all_to_all(copies, axis, split_axis=0, concat_axis=0, tiled=True)  10.4 us
    another operation x6, local copies, waits for them, and re-layouts  6.83 us
  transfers between devices with their start and end apart: 2, of which 2 were waited for; matrix products, arithmetic and copies ran while one was open for 0% of the time, Pallas kernels for 0%

commit v1 on v0

v1 whole, which is shorter than its diff:
```python
import functools

import jax
import jax.numpy as jnp
from jax import lax
from jax.experimental import pallas as pl
from jax.experimental.pallas import tpu as pltpu
from jax.sharding import PartitionSpec as P

HIGH = lax.Precision.HIGHEST
F32 = jnp.float32
BF16 = jnp.bfloat16
MESH = pl.DeviceIdType.MESH
NZ, NY, NX = 8, 4, 4
POINTS, SNAPS, WIDTH = 384, 2048, 256
HALF = WIDTH // 2
SHARE = POINTS // NX
PANEL = 32
TOTAL = 24576


def three_parts(value):
    first = value.astype(BF16)
    rest = value - first.astype(F32)
    second = rest.astype(BF16)
    third = (rest - second.astype(F32)).astype(BF16)
    return first, second, third


def factor_panel(p, g_ref, x_ref):
    top = pl.multiple_of(p * PANEL, PANEL)
    rows = pl.ds(top, PANEL)
    left, right = g_ref[rows, 0:128], g_ref[rows, 128:256]
    own = jnp.where(p < 4, left, right)
    own = pltpu.roll(own, lax.rem(128 - lax.rem(top, 128), 128), 1)
    x_left, x_right = x_ref[rows, 0:128], x_ref[rows, 128:256]
    wide = (left, right, x_left, x_right, own)
    tiles = [[part[8 * g : 8 * g + 8] for part in wide] for g in range(4)]
    sub = lax.broadcasted_iota(jnp.int32, (8, 128), 0)
    for b in range(4):
        column = {}
        for k in range(8):
            for g in range(b, 4):
                lane = tiles[g][4][:, 8 * b + k : 8 * b + k + 1]
                column[g, k] = jnp.broadcast_to(lane, (8, 128))
        for k in range(8):
            scale = lax.rsqrt(jnp.broadcast_to(column[b, k][k : k + 1, :], (8, 128)))
            low = {g: column[g, k] * scale for g in range(b, 4)}
            for m in range(k + 1, 8):
                entry = jnp.broadcast_to(low[b][m : m + 1, :], (8, 128))
                for g in range(b, 4):
                    column[g, m] = column[g, m] - low[g] * entry
            below = jnp.where(sub <= k, 0.0, low[b])
            for w in range(5):
                row = jnp.broadcast_to(tiles[b][w][k : k + 1, :], (8, 128)) * scale
                tiles[b][w] = jnp.where(sub == k, row, tiles[b][w] - below * row)
                for g in range(b + 1, 4):
                    tiles[g][w] = tiles[g][w] - low[g] * row
    for g in range(4):
        lines = pl.ds(top + 8 * g, 8)
        g_ref[lines, 0:128], g_ref[lines, 128:256] = tiles[g][0], tiles[g][1]
        x_ref[lines, 0:128], x_ref[lines, 128:256] = tiles[g][2], tiles[g][3]


def update_below(p, g_ref, x_ref):
    top = pl.multiple_of(p * PANEL, PANEL)
    g, x = g_ref[pl.ds(top, PANEL), :], x_ref[pl.ds(top, PANEL), :]
    lane = lax.broadcasted_iota(jnp.int32, (PANEL, WIDTH), 1)
    a, b, c = three_parts(jnp.where(lane >= top + PANEL, g, 0.0))
    lhs = jnp.concatenate([a, a, b, a, c, b], 0)
    dims = (((0,), (0,)), ((), ()))
    for ref, value in ((g_ref, g), (x_ref, x)):
        a, b, c = three_parts(value)
        rhs = jnp.concatenate([a, b, a, c, a, b], 0)
        ref[...] -= lax.dot_general(lhs, rhs, dims, preferred_element_type=F32)


def kernel(
    a_hbm, t_hbm, z_ref, r_ref, x_ref,
    a_ref, t_ref, at_ref, p_ref, s_ref, rx_ref, zs_ref, zo_ref, rs_ref, ry_ref, zy_ref, rz_ref,
    gf_ref, gs_ref, g1_ref, gy_ref, gz_ref, gm_ref,
    load, xs, xr, xas, xar, ss, sr, ys, yr, zs, zr, zas, zar, yas, yar, sas, sar,
    gss, gsr, gys, gyr, gzs, gzr, gas, gar, gbs, gbr,
):
    row, x = lax.axis_index("rows"), lax.axis_index("cols")
    c, y, z = lax.rem(row, 2), lax.rem(row // 2, NY), row // (2 * NY)

    def at(dz=0, dy=0, dx=0, dc=0):
        zz, yy = lax.rem(z + dz, NZ), lax.rem(y + dy, NY)
        xx, cc = lax.rem(x + dx, NX), lax.rem(c + dc, 2)
        return ((zz * NY + yy) * 2 + cc, xx)

    def remote(src, dst, send, recv, device):
        return pltpu.make_async_remote_copy(
            src_ref=src, dst_ref=dst, send_sem=send, recv_sem=recv, device_id=device, device_id_type=MESH
        )

    def cols(h):
        return pl.ds(h * HALF, HALF)

    flat = [(dx, dy) for dx in range(NX) for dy in range(NY) if dx or dy]

    def load_a(k):
        part = pl.ds(k * 256, 256)
        return pltpu.make_async_copy(a_hbm.at[:, part], a_ref.at[:, part], load.at[0, k])

    def load_t(k):
        part = pl.ds(k * 256, 256)
        return pltpu.make_async_copy(t_hbm.at[part, :], t_ref.at[part, :], load.at[1, k])

    for k in range(8):
        load_a(k).start()
        load_t(k).start()
    barrier = pltpu.get_barrier_semaphore()
    friends = [at(dc=1)] + [at(dz=d) for d in range(1, NZ)] + [at(dx=dx, dy=dy) for dx, dy in flat]
    for friend in friends:
        pl.semaphore_signal(barrier, inc=1, device_id=friend, device_id_type=MESH)

    for k in range(8):
        load_a(k).wait()
        load_t(k).wait()
        part = jnp.dot(
            a_ref[:, k * 256 : k * 256 + 256], t_ref[k * 256 : k * 256 + 256, :],
            precision=HIGH, preferred_element_type=F32,
        )
        for h in range(2):
            piece = part[:, h * HALF : h * HALF + HALF]
            p_ref[h] = piece if k == 0 else p_ref[h] + piece
    pl.semaphore_wait(barrier, len(friends))

    def share(index):
        return pl.ds(pl.multiple_of(index * SHARE, SHARE), SHARE)

    def x_scatter(h, d):
        src = p_ref.at[h, share(lax.rem(x + d, NX))]
        return remote(src, rx_ref.at[h, d - 1], xs.at[h, d - 1], xr.at[h, d - 1], at(dx=d))

    def x_gather(h, d):
        mine = s_ref.at[h, share(x)]
        return remote(mine, mine, xas.at[h, d - 1], xar.at[h, d - 1], at(dx=d))

    for h in range(2):
        for d in (2, 1, 3):
            x_scatter(h, d).start()
    for k in range(8):
        at_ref[k * 256 : k * 256 + 256, :] = a_ref[:, k * 256 : k * 256 + 256].T
    for h in range(2):
        for d in (1, 2, 3):
            x_scatter(h, d).wait_recv()
        s_ref[h, share(x), :] = (p_ref[h, share(x), :] + rx_ref[h, 0]) + (rx_ref[h, 1] + rx_ref[h, 2])
        for d in (2, 1, 3):
            x_gather(h, d).start()

    def cross(h, out_ref, core):
        sketch = s_ref[h]

        @pl.loop(0, 4)
        def _(i):
            lines = pl.ds(pl.multiple_of(core * 1024 + i * 256, 256), 256)
            out_ref[h, pl.ds(pl.multiple_of(i * 256, 256), 256), :] = jnp.dot(
                at_ref[lines, :], sketch, precision=HIGH, preferred_element_type=F32
            )

    def s_scatter(h):
        return remote(zs_ref.at[h], rs_ref.at[h], ss.at[h], sr.at[h], at(dc=1))

    def y_scatter(h, d):
        src = zo_ref.at[h, pl.ds(pl.multiple_of(lax.rem(y + d, NY) * 256, 256), 256)]
        return remote(src, ry_ref.at[h, d - 1], ys.at[h, d - 1], yr.at[h, d - 1], at(dy=d))

    def z_scatter(h, d):
        src = zy_ref.at[h, pl.ds(pl.multiple_of(lax.rem(z + d, NZ) * 32, 32), 32)]
        return remote(src, rz_ref.at[h, d - 1], zs.at[h, d - 1], zr.at[h, d - 1], at(dz=d))

    base_c = pl.multiple_of(c * 1024, 1024)
    base_y = pl.multiple_of(base_c + y * 256, 256)
    base_z = pl.multiple_of(base_y + z * 32, 32)

    def z_gather(h, d):
        mine = z_ref.at[pl.ds(base_z, 32), cols(h)]
        return remote(mine, mine, zas.at[h, d - 1], zar.at[h, d - 1], at(dz=d))

    def y_gather(h, d):
        mine = z_ref.at[pl.ds(base_y, 256), cols(h)]
        return remote(mine, mine, yas.at[h, d - 1], yar.at[h, d - 1], at(dy=d))

    def s_gather(h):
        mine = z_ref.at[pl.ds(base_c, 1024), cols(h)]
        return remote(mine, mine, sas.at[h], sar.at[h], at(dc=1))

    def to_y(h):
        s_scatter(h).wait_recv()
        zo_ref[h] += rs_ref[h]
        for d in (2, 1, 3):
            y_scatter(h, d).start()

    def to_z(h):
        for d in (1, 2, 3):
            y_scatter(h, d).wait_recv()
        own = zo_ref[h, pl.ds(pl.multiple_of(y * 256, 256), 256), :]
        zy_ref[h] = (own + ry_ref[h, 0]) + (ry_ref[h, 1] + ry_ref[h, 2])
        for d in (4, 3, 5, 2, 6, 1, 7):
            z_scatter(h, d).start()

    def back_z(h):
        for d in range(1, NZ):
            z_scatter(h, d).wait_recv()
        total = zy_ref[h, pl.ds(pl.multiple_of(z * 32, 32), 32), :]
        for d in range(1, NZ):
            total = total + rz_ref[h, d - 1]
        z_ref[pl.ds(base_z, 32), h * HALF : h * HALF + HALF] = total
        for d in (4, 3, 5, 2, 6, 1, 7):
            z_gather(h, d).start()

    def back_y(h):
        for d in range(1, NZ):
            z_gather(h, d).wait_recv()
        for d in (2, 1, 3):
            y_gather(h, d).start()

    def back_s(h):
        for d in (1, 2, 3):
            y_gather(h, d).wait_recv()
        s_gather(h).start()

    def gs_scatter():
        src = gf_ref.at[pl.ds(pl.multiple_of(x * 64 + (1 - c) * 32, 32), 32)]
        return remote(src, gs_ref, gss, gsr, at(dc=1))

    def gy_scatter(d):
        src = g1_ref.at[pl.ds(pl.multiple_of(lax.rem(y + d, NY) * 8, 8), 8)]
        return remote(src, gy_ref.at[d - 1], gys.at[d - 1], gyr.at[d - 1], at(dy=d))

    def gz_all(d):
        mine = gz_ref.at[z]
        return remote(mine, mine, gzs.at[d - 1], gzr.at[d - 1], at(dz=d))

    lines_y = pl.ds(pl.multiple_of(y * 8, 8), 8)

    def g_gather(i):
        mine = gm_ref.at[x, c, lines_y]
        return remote(mine, mine, gas.at[i], gar.at[i], at(dx=flat[i][0], dy=flat[i][1]))

    def gb_gather():
        mine = gm_ref.at[:, c]
        return remote(mine, mine, gbs, gbr, at(dc=1))

    for d in (1, 2, 3):
        x_gather(0, d).wait_recv()
    cross(0, zs_ref, 1 - c)
    s_scatter(0).start()
    cross(0, zo_ref, c)
    for d in (1, 2, 3):
        x_gather(1, d).wait_recv()
    whole = jnp.concatenate([s_ref[0], s_ref[1]], 1)
    gf_ref[...] = lax.dot_general(
        whole, whole, (((0,), (0,)), ((), ())), precision=HIGH, preferred_element_type=F32
    )
    gs_scatter().start()
    cross(1, zs_ref, 1 - c)
    s_scatter(1).start()
    gs_scatter().wait_recv()
    g1_ref[...] = gf_ref[pl.ds(pl.multiple_of(x * 64 + c * 32, 32), 32), :] + gs_ref[...]
    for d in (2, 1, 3):
        gy_scatter(d).start()
    to_y(0)
    cross(1, zo_ref, c)
    for d in (1, 2, 3):
        gy_scatter(d).wait_recv()
    gz_ref[z] = (g1_ref[lines_y, :] + gy_ref[0]) + (gy_ref[1] + gy_ref[2])
    for d in (4, 3, 5, 2, 6, 1, 7):
        gz_all(d).start()
    to_y(1)
    for d in range(1, NZ):
        gz_all(d).wait_recv()
    total = gz_ref[0]
    for i in range(1, NZ):
        total = total + gz_ref[i]
    gm_ref[x, c, lines_y, :] = total
    for i in range(len(flat)):
        g_gather(i).start()
    to_z(0)
    for i in range(len(flat)):
        g_gather(i).wait_recv()
    gb_gather().start()
    x_ref[...] = jnp.where(
        lax.broadcasted_iota(jnp.int32, (WIDTH, WIDTH), 0) == lax.broadcasted_iota(jnp.int32, (WIDTH, WIDTH), 1),
        1.0, 0.0,
    )
    gb_gather().wait_recv()
    r_ref[...] = gm_ref[...].reshape(WIDTH, WIDTH)

    hooks = {0: (to_z, 1), 1: (back_z, 0), 2: (back_z, 1), 3: (back_y, 0), 4: (back_y, 1), 6: (back_s, 0)}

    @pl.loop(0, WIDTH // PANEL)
    def _(p):
        for when, (step, h) in hooks.items():
            pl.when(p == when)(functools.partial(step, h))
        factor_panel(p, r_ref, x_ref)
        update_below(p, r_ref, x_ref)

    line = lax.broadcasted_iota(jnp.int32, (WIDTH, WIDTH), 0)
    lane = lax.broadcasted_iota(jnp.int32, (WIDTH, WIDTH), 1)
    r_ref[...] = jnp.where(lane >= line, r_ref[...], 0.0)
    back_s(1)

    gs_scatter().wait_send()
    gb_gather().wait_send()
    for d in (1, 2, 3):
        gy_scatter(d).wait_send()
    for i in range(len(flat)):
        g_gather(i).wait_send()
    for d in range(1, NZ):
        gz_all(d).wait_send()
    for h in range(2):
        for d in (1, 2, 3):
            x_scatter(h, d).wait_send()
            x_gather(h, d).wait_send()
            y_scatter(h, d).wait_send()
            y_gather(h, d).wait_send()
        for d in range(1, NZ):
            z_scatter(h, d).wait_send()
            z_gather(h, d).wait_send()
        s_scatter(h).wait_send()
    for h in range(2):
        s_gather(h).wait()


def body(snapshot, test_matrix):
    dma = pltpu.SemaphoreType.DMA
    hbm = pl.BlockSpec(memory_space=pl.ANY)
    vmem = pl.BlockSpec(memory_space=pltpu.VMEM)
    cross, factor, inverse = pl.pallas_call(
        kernel,
        out_shape=(
            jax.ShapeDtypeStruct((SNAPS, WIDTH), F32),
            jax.ShapeDtypeStruct((WIDTH, WIDTH), F32),
            jax.ShapeDtypeStruct((WIDTH, WIDTH), F32),
        ),
        in_specs=[hbm, hbm],
        out_specs=(vmem, vmem, vmem),
        scratch_shapes=[
            pltpu.VMEM((POINTS, SNAPS), F32),
            pltpu.VMEM((SNAPS, WIDTH), F32),
            pltpu.VMEM((SNAPS, POINTS), F32),
            pltpu.VMEM((2, POINTS, HALF), F32),
            pltpu.VMEM((2, POINTS, HALF), F32),
            pltpu.VMEM((2, 3, SHARE, HALF), F32),
            pltpu.VMEM((2, 1024, HALF), F32),
            pltpu.VMEM((2, 1024, HALF), F32),
            pltpu.VMEM((2, 1024, HALF), F32),
            pltpu.VMEM((2, 3, 256, HALF), F32),
            pltpu.VMEM((2, 256, HALF), F32),
            pltpu.VMEM((2, 7, 32, HALF), F32),
            pltpu.VMEM((WIDTH, WIDTH), F32),
            pltpu.VMEM((32, WIDTH), F32),
            pltpu.VMEM((32, WIDTH), F32),
            pltpu.VMEM((3, 8, WIDTH), F32),
            pltpu.VMEM((8, 8, WIDTH), F32),
            pltpu.VMEM((4, 2, 32, WIDTH), F32),
            dma((2, 8)),
            dma((2, 3)), dma((2, 3)), dma((2, 3)), dma((2, 3)),
            dma((2,)), dma((2,)),
            dma((2, 3)), dma((2, 3)),
            dma((2, 7)), dma((2, 7)), dma((2, 7)), dma((2, 7)),
            dma((2, 3)), dma((2, 3)),
            dma((2,)), dma((2,)),
            dma, dma,
            dma((3,)), dma((3,)),
            dma((7,)), dma((7,)),
            dma((15,)), dma((15,)),
            dma, dma,
        ],
        compiler_params=pltpu.CompilerParams(
            collective_id=0, has_side_effects=True, vmem_limit_bytes=48 * 1024 * 1024
        ),
        name="range_finder",
    )(snapshot, test_matrix)
    projected = lax.dot_general(
        cross, inverse, (((1,), (1,)), ((), ())), precision=HIGH, preferred_element_type=F32
    )
    return projected, factor / jnp.sqrt(jnp.float32(TOTAL))


def solution(mesh):
    return jax.shard_map(
        body,
        mesh=mesh,
        in_specs=(P("rows", "cols"), P("cols", None)),
        out_specs=(P("cols", None), P()),
        check_vma=False,
    )
```

time: 275 us -> 76.2 us (0.28)
  blocking collectives: 105 us -> 0 us
  other arithmetic: 74.2 us -> 0.73 us
  Pallas kernels: 0 us -> 69.9 us
  waiting for transfers between devices: 34.1 us -> 0 us
  local copies, waits for them, and re-layouts: 30.2 us -> 1.58 us
  matrix products: 17.8 us -> 3.15 us
  starting transfers between devices: 10.4 us -> 0 us
    all_to_all x7 -> x0, blocking collectives: 105 us -> none  [the longest x2 52.3 us: summed_rows(): lax.all_to_all(nearer, far, split_axis=0, concat_axis=0, tiled=True)]
    pallas_call x0 -> x1, Pallas kernels: none -> 69.9 us  [body(): pl.pallas_call(kernel, out_shape=(jax.ShapeDtypeStruct((SNAPS, WIDTH), F3...]
    another operation x8 -> x0, other arithmetic: 62.3 us -> none  [the longest x6 41.2 us: body(): lower = jnp.linalg.cholesky(gram)]
    all_to_all x2 -> x0, waiting for transfers between devices: 34.1 us -> none  [copy_for_each(): return lax.all_to_all(copies, axis, split_axis=0, concat_axis=0, tiled=True)]
    another operation x11 -> x0, local copies, waits for them, and re-layouts: 12.6 us -> none
    all_to_all x2 -> x0, starting transfers between devices: 10.4 us -> none  [copy_for_each(): return lax.all_to_all(copies, axis, split_axis=0, concat_axis=0, tiled=True)]
    reduce_sum x5 -> x0, other arithmetic: 9.05 us -> none  [the longest x2 4.46 us: summed_on_arrival(): return arrived.sum(axis=0)]
    dot_general x3 -> x1, matrix products: 10.8 us -> 3.15 us  [body(): lax.dot_general(cross, inverse, (((1,), (1,)), ((), ())), precision=HIGH,...]
  transfers between devices with their start and end apart: 2 -> 0, of which waited for: 2 -> 0; matrix products, arithmetic and copies ran while one was open for 0% -> 0% of each run, Pallas kernels for 0% -> 0%
where the time goes in v1:
time: 76.2 us; the launch traced here: 76.1 us
  Pallas kernels  69.9 us (92%)
  matrix products  3.15 us (4%)
  local copies, waits for them, and re-layouts  1.58 us (2%)
    pallas_call x1, Pallas kernels, body(): pl.pallas_call(kernel, out_shape=(jax.ShapeDtypeStruct((SNAPS, WIDTH), F3...  69.9 us
    dot_general x1, matrix products, body(): lax.dot_general(cross, inverse, (((1,), (1,)), ((), ())), precision=HIGH,...  3.15 us
    unnamed x2, local copies, waits for them, and re-layouts  1.58 us

profile of v1, /device:TPU:1, one launch (start us, length us, event | category | flops | bytes accessed | tf_op | source)
XLA Modules:
  0.0 76.1 jit_solution(5529151385039970353)
XLA Ops:
  0.6 0.0 copy-start
  0.6 1.6 %copy-done = f32[2048,256]{1,0:T(8,128)S(1)} copy-done((f32[2048,256]{1,0:T(8,128)S(1)}, f32[2048,256]{1,0:T(8,128)}, u32[]{:S(2)}) %copy-start) | copy-done | bytes 2097176
  2.2 69.9 %range_finder.1 = (f32[2048,256]{1,0:T(8,128)S(1)}, f32[256,256]{1,0:T(8,128)S(1)}, f32[256,256]{1,0:T(8,128)S(1)}) custom-call(f32[384,2048]{1,0:T(8,128)} %a_hbm.1, f32[2048,256]{1,0:T(8,128)S(1)} %copy-done), custom_call_target="tpu_custom_call" | custom-call | tf_op jit(solution)/shard_map/range_finder/pallas_call | solution.py:333
  72.2 3.2 %fusion = f32[2048,256]{1,0:T(8,128)} fusion(f32[2048,256]{1,0:T(8,128)S(1)} %get-tuple-element.5, f32[256,256]{1,0:T(8,128)S(1)} %get-tuple-element.6), kind=kOutput, calls=%fused_computation.1 | convolution fusion | flops 1610612736 | bytes 4456448 | tf_op jit(solution)/shard_map/dot_general | solution.py:379
  75.3 0.7 broadcast_multiply_fusion
Async XLA Ops:
  0.6 1.6 %copy-start = (f32[2048,256]{1,0:T(8,128)S(1)}, f32[2048,256]{1,0:T(8,128)}, u32[]{:S(2)}) copy-start(f32[2048,256]{1,0:T(8,128)} %t_hbm.1) | copy-start | bytes 6291460

commit v2 on v1

--- a/solution.py
+++ b/solution.py
@@ -75,6 +75,38 @@
         ref[...] -= lax.dot_general(lhs, rhs, dims, preferred_element_type=F32)
 
 
+class Copies:
+    def __init__(self):
+        self.open = {}
+
+    def tracked(self, make):
+        return lambda *where: Copy(self.open, make, where)
+
+    def drain(self):
+        for (make, where), sides in self.open.items():
+            copy = make(*where)
+            for side in sides:
+                getattr(copy, side)()
+        self.open = {}
+
+
+class Copy:
+    def __init__(self, open_copies, make, where):
+        self.open, self.key, self.copy = open_copies, (make, where), make(*where)
+
+    def start(self):
+        self.copy.start()
+        self.open[self.key] = ["wait_recv", "wait_send"]
+
+    def wait_recv(self):
+        self.copy.wait_recv()
+        self.open[self.key].remove("wait_recv")
+
+    def wait_send(self):
+        self.copy.wait_send()
+        self.open[self.key].remove("wait_send")
+
+
 def kernel(
     a_hbm, t_hbm, z_ref, r_ref, x_ref,
     a_ref, t_ref, at_ref, p_ref, s_ref, rx_ref, zs_ref, zo_ref, rs_ref, ry_ref, zy_ref, rz_ref,
@@ -100,6 +132,9 @@
 
     flat = [(dx, dy) for dx in range(NX) for dy in range(NY) if dx or dy]
 
+    copies = Copies()
+    tracked = copies.tracked
+
     def load_a(k):
         part = pl.ds(k * 256, 256)
         return pltpu.make_async_copy(a_hbm.at[:, part], a_ref.at[:, part], load.at[0, k])
@@ -116,32 +151,41 @@
     for friend in friends:
         pl.semaphore_signal(barrier, inc=1, device_id=friend, device_id_type=MESH)
 
-    for k in range(8):
-        load_a(k).wait()
-        load_t(k).wait()
-        part = jnp.dot(
-            a_ref[:, k * 256 : k * 256 + 256], t_ref[k * 256 : k * 256 + 256, :],
-            precision=HIGH, preferred_element_type=F32,
-        )
-        for h in range(2):
-            piece = part[:, h * HALF : h * HALF + HALF]
-            p_ref[h] = piece if k == 0 else p_ref[h] + piece
-    pl.semaphore_wait(barrier, len(friends))
-
     def share(index):
         return pl.ds(pl.multiple_of(index * SHARE, SHARE), SHARE)
 
+    @tracked
     def x_scatter(h, d):
         src = p_ref.at[h, share(lax.rem(x + d, NX))]
         return remote(src, rx_ref.at[h, d - 1], xs.at[h, d - 1], xr.at[h, d - 1], at(dx=d))
 
+    for group in ((2, 1), (3, 0)):
+        for k in range(8):
+            if group[0] == 2:
+                load_a(k).wait()
+                load_t(k).wait()
+            lines = [share(lax.rem(x + d, NX)) for d in group]
+            part = jnp.dot(
+                jnp.concatenate([a_ref[line, k * 256 : k * 256 + 256] for line in lines], 0),
+                t_ref[k * 256 : k * 256 + 256, :],
+                precision=HIGH, preferred_element_type=F32,
+            )
+            for i, line in enumerate(lines):
+                for h in range(2):
+                    piece = part[i * SHARE : i * SHARE + SHARE, h * HALF : h * HALF + HALF]
+                    p_ref[h, line, :] = piece if k == 0 else p_ref[h, line, :] + piece
+        if group[0] == 2:
+            pl.semaphore_wait(barrier, len(friends))
+        for h in range(2):
+            for d in group:
+                if d:
+                    x_scatter(h, d).start()
+
+    @tracked
     def x_gather(h, d):
         mine = s_ref.at[h, share(x)]
         return remote(mine, mine, xas.at[h, d - 1], xar.at[h, d - 1], at(dx=d))
 
-    for h in range(2):
-        for d in (2, 1, 3):
-            x_scatter(h, d).start()
     for k in range(8):
         at_ref[k * 256 : k * 256 + 256, :] = a_ref[:, k * 256 : k * 256 + 256].T
     for h in range(2):
@@ -161,86 +205,112 @@
                 at_ref[lines, :], sketch, precision=HIGH, preferred_element_type=F32
             )
 
+    @tracked
     def s_scatter(h):
         return remote(zs_ref.at[h], rs_ref.at[h], ss.at[h], sr.at[h], at(dc=1))
 
-    def y_scatter(h, d):
-        src = zo_ref.at[h, pl.ds(pl.multiple_of(lax.rem(y + d, NY) * 256, 256), 256)]
-        return remote(src, ry_ref.at[h, d - 1], ys.at[h, d - 1], yr.at[h, d - 1], at(dy=d))
-
-    def z_scatter(h, d):
-        src = zy_ref.at[h, pl.ds(pl.multiple_of(lax.rem(z + d, NZ) * 32, 32), 32)]
-        return remote(src, rz_ref.at[h, d - 1], zs.at[h, d - 1], zr.at[h, d - 1], at(dz=d))
-
-    base_c = pl.multiple_of(c * 1024, 1024)
-    base_y = pl.multiple_of(base_c + y * 256, 256)
-    base_z = pl.multiple_of(base_y + z * 32, 32)
-
-    def z_gather(h, d):
-        mine = z_ref.at[pl.ds(base_z, 32), cols(h)]
-        return remote(mine, mine, zas.at[h, d - 1], zar.at[h, d - 1], at(dz=d))
-
-    def y_gather(h, d):
-        mine = z_ref.at[pl.ds(base_y, 256), cols(h)]
-        return remote(mine, mine, yas.at[h, d - 1], yar.at[h, d - 1], at(dy=d))
-
-    def s_gather(h):
-        mine = z_ref.at[pl.ds(base_c, 1024), cols(h)]
-        return remote(mine, mine, sas.at[h], sar.at[h], at(dc=1))
+    pair, bit = z // 2, lax.rem(z, 2)
+    FAR = (2, 1, 3, 0)
+
+    def further(s, t):
+        return 2 * lax.rem(pair + s, 4) + lax.rem(bit + t, 2)
+
+    def block(index, size):
+        return pl.ds(pl.multiple_of(index * size, size), size)
+
+    def others(s):
+        return (1,) if s == 0 else (0, 1)
+
+    @tracked
+    def y_scatter(h, s, d):
+        part = lax.rem(pair + s, 4)
+        src = zo_ref.at[h, block(lax.rem(y + d, NY) * 4 + part, 64)]
+        return remote(src, ry_ref.at[h, d - 1, block(part, 64)], ys.at[h, s, d - 1], yr.at[h, s, d - 1], at(dy=d))
+
+    @tracked
+    def z_scatter(h, s, t):
+        src = zy_ref.at[h, block(further(s, t), 32)]
+        i = 2 * s + t - 1
+        return remote(src, rz_ref.at[h, i], zs.at[h, i], zr.at[h, i], at(dz=further(s, t) - z + NZ))
+
+    @tracked
+    def z_gather(h, s, t):
+        mine = z_ref.at[c, y, block(z, 32), cols(h)]
+        i = 2 * s + t - 1
+        return remote(mine, mine, zas.at[h, i], zar.at[h, i], at(dz=further(s, t) - z + NZ))
+
+    @tracked
+    def y_gather(h, s, d):
+        mine = z_ref.at[c, y, block(lax.rem(pair - s + 4, 4), 64), cols(h)]
+        return remote(mine, mine, yas.at[h, s, d - 1], yar.at[h, s, d - 1], at(dy=d))
+
+    @tracked
+    def s_gather(h, s):
+        mine = z_ref.at[c, :, block(lax.rem(pair - s + 4, 4), 64), cols(h)]
+        return remote(mine, mine, sas.at[h, s], sar.at[h, s], at(dc=1))
 
     def to_y(h):
         s_scatter(h).wait_recv()
         zo_ref[h] += rs_ref[h]
+        for s in FAR:
+            for d in (2, 1, 3):
+                y_scatter(h, s, d).start()
+
+    def to_z(h, s):
+        for d in (1, 2, 3):
+            y_scatter(h, s, d).wait_recv()
+        part = lax.rem(pair + s, 4)
+        lines = block(part, 64)
+        own = zo_ref[h, block(y * 4 + part, 64), :]
+        zy_ref[h, lines, :] = (own + ry_ref[h, 0, lines, :]) + (ry_ref[h, 1, lines, :] + ry_ref[h, 2, lines, :])
+        for t in others(s):
+            z_scatter(h, s, t).start()
+
+    def back_z(h):
+        total = zy_ref[h, block(z, 32), :]
+        for s in (0, 1, 3, 2):
+            for t in others(s):
+                z_scatter(h, s, t).wait_recv()
+                total = total + rz_ref[h, 2 * s + t - 1]
+        z_ref[c, y, block(z, 32), h * HALF : h * HALF + HALF] = total
+        for s in FAR:
+            for t in others(s):
+                z_gather(h, s, t).start()
+
+    def back_y(h, s):
+        for t in others(s):
+            z_gather(h, s, t).wait_recv()
         for d in (2, 1, 3):
-            y_scatter(h, d).start()
-
-    def to_z(h):
+            y_gather(h, s, d).start()
+
+    def back_s(h, s):
         for d in (1, 2, 3):
-            y_scatter(h, d).wait_recv()
-        own = zo_ref[h, pl.ds(pl.multiple_of(y * 256, 256), 256), :]
-        zy_ref[h] = (own + ry_ref[h, 0]) + (ry_ref[h, 1] + ry_ref[h, 2])
-        for d in (4, 3, 5, 2, 6, 1, 7):
-            z_scatter(h, d).start()
-
-    def back_z(h):
-        for d in range(1, NZ):
-            z_scatter(h, d).wait_recv()
-        total = zy_ref[h, pl.ds(pl.multiple_of(z * 32, 32), 32), :]
-        for d in range(1, NZ):
-            total = total + rz_ref[h, d - 1]
-        z_ref[pl.ds(base_z, 32), h * HALF : h * HALF + HALF] = total
-        for d in (4, 3, 5, 2, 6, 1, 7):
-            z_gather(h, d).start()
-
-    def back_y(h):
-        for d in range(1, NZ):
-            z_gather(h, d).wait_recv()
-        for d in (2, 1, 3):
-            y_gather(h, d).start()
-
-    def back_s(h):
-        for d in (1, 2, 3):
-            y_gather(h, d).wait_recv()
-        s_gather(h).start()
-
+            y_gather(h, s, d).wait_recv()
+        s_gather(h, s).start()
+
+    @tracked
     def gs_scatter():
         src = gf_ref.at[pl.ds(pl.multiple_of(x * 64 + (1 - c) * 32, 32), 32)]
         return remote(src, gs_ref, gss, gsr, at(dc=1))
 
+    @tracked
     def gy_scatter(d):
         src = g1_ref.at[pl.ds(pl.multiple_of(lax.rem(y + d, NY) * 8, 8), 8)]
         return remote(src, gy_ref.at[d - 1], gys.at[d - 1], gyr.at[d - 1], at(dy=d))
 
+    @tracked
     def gz_all(d):
         mine = gz_ref.at[z]
         return remote(mine, mine, gzs.at[d - 1], gzr.at[d - 1], at(dz=d))
 
     lines_y = pl.ds(pl.multiple_of(y * 8, 8), 8)
 
+    @tracked
     def g_gather(i):
         mine = gm_ref.at[x, c, lines_y]
         return remote(mine, mine, gas.at[i], gar.at[i], at(dx=flat[i][0], dy=flat[i][1]))
 
+    @tracked
     def gb_gather():
         mine = gm_ref.at[:, c]
         return remote(mine, mine, gbs, gbr, at(dc=1))
@@ -257,20 +327,22 @@
         whole, whole, (((0,), (0,)), ((), ())), precision=HIGH, preferred_element_type=F32
     )
     gs_scatter().start()
+    to_y(0)
     cross(1, zs_ref, 1 - c)
     s_scatter(1).start()
     gs_scatter().wait_recv()
     g1_ref[...] = gf_ref[pl.ds(pl.multiple_of(x * 64 + c * 32, 32), 32), :] + gs_ref[...]
     for d in (2, 1, 3):
         gy_scatter(d).start()
-    to_y(0)
     cross(1, zo_ref, c)
+    to_y(1)
     for d in (1, 2, 3):
         gy_scatter(d).wait_recv()
     gz_ref[z] = (g1_ref[lines_y, :] + gy_ref[0]) + (gy_ref[1] + gy_ref[2])
     for d in (4, 3, 5, 2, 6, 1, 7):
         gz_all(d).start()
-    to_y(1)
+    for s in FAR:
+        to_z(0, s)
     for d in range(1, NZ):
         gz_all(d).wait_recv()
     total = gz_ref[0]
@@ -279,61 +351,56 @@
     gm_ref[x, c, lines_y, :] = total
     for i in range(len(flat)):
         g_gather(i).start()
-    to_z(0)
-    for i in range(len(flat)):
-        g_gather(i).wait_recv()
-    gb_gather().start()
     x_ref[...] = jnp.where(
         lax.broadcasted_iota(jnp.int32, (WIDTH, WIDTH), 0) == lax.broadcasted_iota(jnp.int32, (WIDTH, WIDTH), 1),
         1.0, 0.0,
     )
+    for s in FAR:
+        to_z(1, s)
+    back_z(0)
+    for s in (0, 1, 3, 2):
+        back_y(0, s)
+    for i in range(len(flat)):
+        g_gather(i).wait_recv()
+    gb_gather().start()
     gb_gather().wait_recv()
     r_ref[...] = gm_ref[...].reshape(WIDTH, WIDTH)
 
-    hooks = {0: (to_z, 1), 1: (back_z, 0), 2: (back_z, 1), 3: (back_y, 0), 4: (back_y, 1), 6: (back_s, 0)}
+    hooks = {
+        0: ((back_z, 1),),
+        3: ((back_y, 1, 0), (back_y, 1, 1), (back_y, 1, 3), (back_y, 1, 2)),
+        5: ((back_s, 0, 0), (back_s, 0, 1), (back_s, 0, 3), (back_s, 0, 2)),
+    }
 
     @pl.loop(0, WIDTH // PANEL)
     def _(p):
-        for when, (step, h) in hooks.items():
-            pl.when(p == when)(functools.partial(step, h))
+        for when, steps in hooks.items():
+
+            @pl.when(p == when)
+            def _():
+                for step, *where in steps:
+                    step(*where)
+
         factor_panel(p, r_ref, x_ref)
         update_below(p, r_ref, x_ref)
 
     line = lax.broadcasted_iota(jnp.int32, (WIDTH, WIDTH), 0)
     lane = lax.broadcasted_iota(jnp.int32, (WIDTH, WIDTH), 1)
     r_ref[...] = jnp.where(lane >= line, r_ref[...], 0.0)
-    back_s(1)
-
-    gs_scatter().wait_send()
-    gb_gather().wait_send()
-    for d in (1, 2, 3):
-        gy_scatter(d).wait_send()
-    for i in range(len(flat)):
-        g_gather(i).wait_send()
-    for d in range(1, NZ):
-        gz_all(d).wait_send()
-    for h in range(2):
-        for d in (1, 2, 3):
-            x_scatter(h, d).wait_send()
-            x_gather(h, d).wait_send()
-            y_scatter(h, d).wait_send()
-            y_gather(h, d).wait_send()
-        for d in range(1, NZ):
-            z_scatter(h, d).wait_send()
-            z_gather(h, d).wait_send()
-        s_scatter(h).wait_send()
-    for h in range(2):
-        s_gather(h).wait()
+    for s in (0, 1, 3, 2):
+        back_s(1, s)
+
+    copies.drain()
 
 
 def body(snapshot, test_matrix):
     dma = pltpu.SemaphoreType.DMA
-    hbm = pl.BlockSpec(memory_space=pl.ANY)
+    hbm = pl.BlockSpec(memory_space=pltpu.HBM)
     vmem = pl.BlockSpec(memory_space=pltpu.VMEM)
     cross, factor, inverse = pl.pallas_call(
         kernel,
         out_shape=(
-            jax.ShapeDtypeStruct((SNAPS, WIDTH), F32),
+            jax.ShapeDtypeStruct((2, NY, 256, WIDTH), F32),
             jax.ShapeDtypeStruct((WIDTH, WIDTH), F32),
             jax.ShapeDtypeStruct((WIDTH, WIDTH), F32),
         ),
@@ -361,10 +428,10 @@
             dma((2, 8)),
             dma((2, 3)), dma((2, 3)), dma((2, 3)), dma((2, 3)),
             dma((2,)), dma((2,)),
-            dma((2, 3)), dma((2, 3)),
+            dma((2, 4, 3)), dma((2, 4, 3)),
             dma((2, 7)), dma((2, 7)), dma((2, 7)), dma((2, 7)),
-            dma((2, 3)), dma((2, 3)),
-            dma((2,)), dma((2,)),
+            dma((2, 4, 3)), dma((2, 4, 3)),
+            dma((2, 4)), dma((2, 4)),
             dma, dma,
             dma((3,)), dma((3,)),
             dma((7,)), dma((7,)),
@@ -375,9 +442,9 @@
             collective_id=0, has_side_effects=True, vmem_limit_bytes=48 * 1024 * 1024
         ),
         name="range_finder",
-    )(snapshot, test_matrix)
+    )(*(pltpu.with_memory_space_constraint(value, pltpu.HBM) for value in (snapshot, test_matrix)))
     projected = lax.dot_general(
-        cross, inverse, (((1,), (1,)), ((), ())), precision=HIGH, preferred_element_type=F32
+        cross.reshape(SNAPS, WIDTH), inverse, (((1,), (1,)), ((), ())), precision=HIGH, preferred_element_type=F32
     )
     return projected, factor / jnp.sqrt(jnp.float32(TOTAL))
 

time: 76.2 us -> 69 us (0.906)
  Pallas kernels: 69.9 us -> 64.4 us
  local copies, waits for them, and re-layouts: 1.58 us -> 0 us
    pallas_call x1, Pallas kernels: 69.9 us -> 64.4 us  [body(): pl.pallas_call(kernel, out_shape=(jax.ShapeDtypeStruct((2, NY, 256, WIDTH...]
    unnamed x2 -> x0, local copies, waits for them, and re-layouts: 1.58 us -> none
where the time goes in v2:
time: 69 us; the launch traced here: 68.9 us
  Pallas kernels  64.4 us (93%)
  matrix products  3.16 us (5%)
  other arithmetic  0.73 us (1%)
    pallas_call x1, Pallas kernels, body(): pl.pallas_call(kernel, out_shape=(jax.ShapeDtypeStruct((2, NY, 256, WIDTH...  64.4 us
    dot_general x1, matrix products, body(): lax.dot_general(cross.reshape(SNAPS, WIDTH), inverse, (((1,), (1,)), ((),...  3.16 us

profile of v2, /device:TPU:1, one launch (start us, length us, event | category | flops | bytes accessed | tf_op | source)
XLA Modules:
  0.0 68.9 jit_solution(2943713969505642485)
XLA Ops:
  0.6 64.4 %range_finder.1 = (f32[2,4,256,256]{3,2,1,0:T(8,128)S(1)}, f32[256,256]{1,0:T(8,128)S(1)}, f32[256,256]{1,0:T(8,128)S(1)}) custom-call(f32[384,2048]{1,0:T(8,128)} %a_hbm.1, f32[2048,256]{1,0:T(8,128)} %t_hbm.1), custom_call_target="tpu_custom_call" | custom-call | tf_op jit(solution)/shard_map/range_finder/pallas_call | solution.py:400
  65.0 3.2 %fusion = f32[2048,256]{1,0:T(8,128)} fusion(f32[2048,256]{1,0:T(8,128)S(1)} %bitcast.3, f32[256,256]{1,0:T(8,128)S(1)} %get-tuple-element.6), kind=kOutput, calls=%fused_computation.1 | convolution fusion | flops 1610612736 | bytes 4456448 | tf_op jit(solution)/shard_map/dot_general | solution.py:446
  68.2 0.7 %broadcast_multiply_fusion = f32[256,256]{1,0:T(8,128)} fusion(f32[256,256]{1,0:T(8,128)S(1)} %get-tuple-element.7), kind=kLoop, calls=%fused_computation | loop fusion | flops 65536 | bytes 524288 | tf_op jit(solution)/shard_map/div | solution.py:449

commit v3 on v2

--- a/solution.py
+++ b/solution.py
@@ -112,7 +112,7 @@
     a_ref, t_ref, at_ref, p_ref, s_ref, rx_ref, zs_ref, zo_ref, rs_ref, ry_ref, zy_ref, rz_ref,
     gf_ref, gs_ref, g1_ref, gy_ref, gz_ref, gm_ref,
     load, xs, xr, xas, xar, ss, sr, ys, yr, zs, zr, zas, zar, yas, yar, sas, sar,
-    gss, gsr, gys, gyr, gzs, gzr, gas, gar, gbs, gbr,
+    gss, gsr, gys, gyr, gzs, gzr, gas, gar, gcs, gcr, gbs, gbr,
 ):
     row, x = lax.axis_index("rows"), lax.axis_index("cols")
     c, y, z = lax.rem(row, 2), lax.rem(row // 2, NY), row // (2 * NY)
@@ -127,11 +127,6 @@
             src_ref=src, dst_ref=dst, send_sem=send, recv_sem=recv, device_id=device, device_id_type=MESH
         )
 
-    def cols(h):
-        return pl.ds(h * HALF, HALF)
-
-    flat = [(dx, dy) for dx in range(NX) for dy in range(NY) if dx or dy]
-
     copies = Copies()
     tracked = copies.tracked
 
@@ -147,7 +142,7 @@
         load_a(k).start()
         load_t(k).start()
     barrier = pltpu.get_barrier_semaphore()
-    friends = [at(dc=1)] + [at(dz=d) for d in range(1, NZ)] + [at(dx=dx, dy=dy) for dx, dy in flat]
+    friends = [at(dc=1)] + [at(dz=d) for d in range(1, NZ)] + [at(dy=d) for d in (1, 2, 3)] + [at(dx=d) for d in (1, 2, 3)]
     for friend in friends:
         pl.semaphore_signal(barrier, inc=1, device_id=friend, device_id_type=MESH)
 
@@ -235,18 +230,18 @@
 
     @tracked
     def z_gather(h, s, t):
-        mine = z_ref.at[c, y, block(z, 32), cols(h)]
+        mine = z_ref.at[h, c, y, block(z, 32)]
         i = 2 * s + t - 1
         return remote(mine, mine, zas.at[h, i], zar.at[h, i], at(dz=further(s, t) - z + NZ))
 
     @tracked
     def y_gather(h, s, d):
-        mine = z_ref.at[c, y, block(lax.rem(pair - s + 4, 4), 64), cols(h)]
+        mine = z_ref.at[h, c, y, block(lax.rem(pair - s + 4, 4), 64)]
         return remote(mine, mine, yas.at[h, s, d - 1], yar.at[h, s, d - 1], at(dy=d))
 
     @tracked
     def s_gather(h, s):
-        mine = z_ref.at[c, :, block(lax.rem(pair - s + 4, 4), 64), cols(h)]
+        mine = z_ref.at[h, c, :, block(lax.rem(pair - s + 4, 4), 64)]
         return remote(mine, mine, sas.at[h, s], sar.at[h, s], at(dc=1))
 
     def to_y(h):
@@ -272,7 +267,7 @@
             for t in others(s):
                 z_scatter(h, s, t).wait_recv()
                 total = total + rz_ref[h, 2 * s + t - 1]
-        z_ref[c, y, block(z, 32), h * HALF : h * HALF + HALF] = total
+        z_ref[h, c, y, block(z, 32), :] = total
         for s in FAR:
             for t in others(s):
                 z_gather(h, s, t).start()
@@ -294,21 +289,24 @@
         return remote(src, gs_ref, gss, gsr, at(dc=1))
 
     @tracked
-    def gy_scatter(d):
-        src = g1_ref.at[pl.ds(pl.multiple_of(lax.rem(y + d, NY) * 8, 8), 8)]
-        return remote(src, gy_ref.at[d - 1], gys.at[d - 1], gyr.at[d - 1], at(dy=d))
-
-    @tracked
-    def gz_all(d):
-        mine = gz_ref.at[z]
-        return remote(mine, mine, gzs.at[d - 1], gzr.at[d - 1], at(dz=d))
-
-    lines_y = pl.ds(pl.multiple_of(y * 8, 8), 8)
-
-    @tracked
-    def g_gather(i):
-        mine = gm_ref.at[x, c, lines_y]
-        return remote(mine, mine, gas.at[i], gar.at[i], at(dx=flat[i][0], dy=flat[i][1]))
+    def gz_scatter(d):
+        src = g1_ref.at[lax.rem(z + d, NZ)]
+        return remote(src, gz_ref.at[d - 1], gzs.at[d - 1], gzr.at[d - 1], at(dz=d))
+
+    @tracked
+    def gy_all(d):
+        mine = gy_ref.at[y]
+        return remote(mine, mine, gys.at[d - 1], gyr.at[d - 1], at(dy=d))
+
+    @tracked
+    def gx_gather(d):
+        mine = gm_ref.at[x, c, z]
+        return remote(mine, mine, gas.at[d - 1], gar.at[d - 1], at(dx=d))
+
+    @tracked
+    def gz_gather(d):
+        mine = gm_ref.at[:, c, z]
+        return remote(mine, mine, gcs.at[d - 1], gcr.at[d - 1], at(dz=d))
 
     @tracked
     def gb_gather():
@@ -330,46 +328,56 @@
     to_y(0)
     cross(1, zs_ref, 1 - c)
     s_scatter(1).start()
-    gs_scatter().wait_recv()
-    g1_ref[...] = gf_ref[pl.ds(pl.multiple_of(x * 64 + c * 32, 32), 32), :] + gs_ref[...]
-    for d in (2, 1, 3):
-        gy_scatter(d).start()
-    cross(1, zo_ref, c)
-    to_y(1)
-    for d in (1, 2, 3):
-        gy_scatter(d).wait_recv()
-    gz_ref[z] = (g1_ref[lines_y, :] + gy_ref[0]) + (gy_ref[1] + gy_ref[2])
-    for d in (4, 3, 5, 2, 6, 1, 7):
-        gz_all(d).start()
-    for s in FAR:
-        to_z(0, s)
-    for d in range(1, NZ):
-        gz_all(d).wait_recv()
-    total = gz_ref[0]
-    for i in range(1, NZ):
-        total = total + gz_ref[i]
-    gm_ref[x, c, lines_y, :] = total
-    for i in range(len(flat)):
-        g_gather(i).start()
     x_ref[...] = jnp.where(
         lax.broadcasted_iota(jnp.int32, (WIDTH, WIDTH), 0) == lax.broadcasted_iota(jnp.int32, (WIDTH, WIDTH), 1),
         1.0, 0.0,
     )
-    for s in FAR:
-        to_z(1, s)
+    gs_scatter().wait_recv()
+    total = gf_ref[pl.ds(pl.multiple_of(x * 64 + c * 32, 32), 32), :] + gs_ref[...]
+    for i in range(2):
+        g1_ref[4 * i : 4 * i + 4] = total[:, i * HALF : i * HALF + HALF].reshape(4, 8, HALF)
+    for d in (4, 3, 5, 2, 6, 1, 7):
+        gz_scatter(d).start()
+    cross(1, zo_ref, c)
+    to_z(0, 2)
+    total = g1_ref[z]
+    for d in range(1, NZ):
+        gz_scatter(d).wait_recv()
+        total = total + gz_ref[d - 1]
+    gy_ref[y] = total
+    for d in (2, 1, 3):
+        gy_all(d).start()
+    to_y(1)
+    for s in (1, 3, 0):
+        to_z(0, s)
+    for d in (1, 2, 3):
+        gy_all(d).wait_recv()
+    gm_ref[x, c, z] = (gy_ref[0] + gy_ref[1]) + (gy_ref[2] + gy_ref[3])
+    for d in (2, 1, 3):
+        gx_gather(d).start()
+    to_z(1, 2)
+    to_z(1, 1)
+    for d in (1, 2, 3):
+        gx_gather(d).wait_recv()
+    for d in (4, 3, 5, 2, 6, 1, 7):
+        gz_gather(d).start()
     back_z(0)
-    for s in (0, 1, 3, 2):
-        back_y(0, s)
-    for i in range(len(flat)):
-        g_gather(i).wait_recv()
+    to_z(1, 3)
+    to_z(1, 0)
+    for d in range(1, NZ):
+        gz_gather(d).wait_recv()
     gb_gather().start()
+    back_y(0, 0)
     gb_gather().wait_recv()
-    r_ref[...] = gm_ref[...].reshape(WIDTH, WIDTH)
+    for i in range(2):
+        r_ref[:, i * HALF : i * HALF + HALF] = gm_ref[:, :, 4 * i : 4 * i + 4].reshape(WIDTH, HALF)
 
     hooks = {
-        0: ((back_z, 1),),
-        3: ((back_y, 1, 0), (back_y, 1, 1), (back_y, 1, 3), (back_y, 1, 2)),
-        5: ((back_s, 0, 0), (back_s, 0, 1), (back_s, 0, 3), (back_s, 0, 2)),
+        0: ((back_y, 0, 1), (back_y, 0, 3)),
+        1: ((back_y, 0, 2), (back_z, 1)),
+        4: ((back_y, 1, 0), (back_y, 1, 1), (back_y, 1, 3)),
+        5: ((back_y, 1, 2), (back_s, 0, 0)),
+        7: ((back_s, 0, 1), (back_s, 0, 3), (back_s, 0, 2)),
     }
 
     @pl.loop(0, WIDTH // PANEL)
@@ -387,10 +395,27 @@
     line = lax.broadcasted_iota(jnp.int32, (WIDTH, WIDTH), 0)
     lane = lax.broadcasted_iota(jnp.int32, (WIDTH, WIDTH), 1)
     r_ref[...] = jnp.where(lane >= line, r_ref[...], 0.0)
+    x_ref[...] = x_ref[...].T
     for s in (0, 1, 3, 2):
         back_s(1, s)
 
     copies.drain()
+
+
+def finish(z_ref, w_ref, r_ref, out_hbm, triangle_hbm, out_ref, triangle_ref, sem):
+    triangle_ref[...] = r_ref[...] * (TOTAL**-0.5)
+    copies = [pltpu.make_async_copy(triangle_ref, triangle_hbm, sem.at[4])]
+    copies[0].start()
+    for i in range(4):
+        lines = pl.ds(i * 512, 512)
+        out_ref[lines, :] = jnp.dot(
+            jnp.concatenate([z_ref[0, lines, :], z_ref[1, lines, :]], 1), w_ref[...],
+            precision=HIGH, preferred_element_type=F32,
+        )
+        copies.append(pltpu.make_async_copy(out_ref.at[lines], out_hbm.at[lines], sem.at[i]))
+        copies[-1].start()
+    for copy in copies:
+        copy.wait()
 
 
 def body(snapshot, test_matrix):
@@ -400,7 +425,7 @@
     cross, factor, inverse = pl.pallas_call(
         kernel,
         out_shape=(
-            jax.ShapeDtypeStruct((2, NY, 256, WIDTH), F32),
+            jax.ShapeDtypeStruct((2, 2, NY, 256, HALF), F32),
             jax.ShapeDtypeStruct((WIDTH, WIDTH), F32),
             jax.ShapeDtypeStruct((WIDTH, WIDTH), F32),
         ),
@@ -421,10 +446,10 @@
             pltpu.VMEM((2, 7, 32, HALF), F32),
             pltpu.VMEM((WIDTH, WIDTH), F32),
             pltpu.VMEM((32, WIDTH), F32),
-            pltpu.VMEM((32, WIDTH), F32),
-            pltpu.VMEM((3, 8, WIDTH), F32),
-            pltpu.VMEM((8, 8, WIDTH), F32),
-            pltpu.VMEM((4, 2, 32, WIDTH), F32),
+            pltpu.VMEM((8, 8, HALF), F32),
+            pltpu.VMEM((4, 8, HALF), F32),
+            pltpu.VMEM((7, 8, HALF), F32),
+            pltpu.VMEM((4, 2, 8, 8, HALF), F32),
             dma((2, 8)),
             dma((2, 3)), dma((2, 3)), dma((2, 3)), dma((2, 3)),
             dma((2,)), dma((2,)),
@@ -435,7 +460,8 @@
             dma, dma,
             dma((3,)), dma((3,)),
             dma((7,)), dma((7,)),
-            dma((15,)), dma((15,)),
+            dma((3,)), dma((3,)),
+            dma((7,)), dma((7,)),
             dma, dma,
         ],
         compiler_params=pltpu.CompilerParams(
@@ -443,10 +469,22 @@
         ),
         name="range_finder",
     )(*(pltpu.with_memory_space_constraint(value, pltpu.HBM) for value in (snapshot, test_matrix)))
-    projected = lax.dot_general(
-        cross.reshape(SNAPS, WIDTH), inverse, (((1,), (1,)), ((), ())), precision=HIGH, preferred_element_type=F32
-    )
-    return projected, factor / jnp.sqrt(jnp.float32(TOTAL))
+    return pl.pallas_call(
+        finish,
+        out_shape=(
+            jax.ShapeDtypeStruct((SNAPS, WIDTH), F32),
+            jax.ShapeDtypeStruct((WIDTH, WIDTH), F32),
+        ),
+        in_specs=[vmem, vmem, vmem],
+        out_specs=(hbm, hbm),
+        scratch_shapes=[
+            pltpu.VMEM((SNAPS, WIDTH), F32),
+            pltpu.VMEM((WIDTH, WIDTH), F32),
+            dma((5,)),
+        ],
+        compiler_params=pltpu.CompilerParams(vmem_limit_bytes=16 * 1024 * 1024),
+        name="final_product",
+    )(cross.reshape(2, SNAPS, HALF), inverse, factor)
 
 
 def solution(mesh):

time: 69 us -> 68.5 us (level)
  Pallas kernels: 64.4 us -> 67.8 us
  matrix products: 3.16 us -> 0 us
  other arithmetic: 0.73 us -> 0 us
    pallas_call x1 -> x2, Pallas kernels: 64.4 us -> 67.8 us  [the longest x1 64.8 us: body(): pl.pallas_call(kernel, out_shape=(jax.ShapeDtypeStruct((2, 2, NY, 256, HA...]
    dot_general x1 -> x0, matrix products: 3.16 us -> none  [body(): lax.dot_general(cross.reshape(SNAPS, WIDTH), inverse, (((1,), (1,)), ((),...]
    div x1 -> x0, other arithmetic: 0.73 us -> none  [body(): return (projected, factor / jnp.sqrt(jnp.float32(TOTAL)))]
where the time goes in v3:
time: 68.5 us; the launch traced here: 68.4 us
  Pallas kernels  67.8 us (99%)
    pallas_call x1, Pallas kernels, body(): pl.pallas_call(kernel, out_shape=(jax.ShapeDtypeStruct((2, 2, NY, 256, HA...  64.8 us
    pallas_call x1, Pallas kernels, body(): pl.pallas_call(finish, out_shape=(jax.ShapeDtypeStruct((SNAPS, WIDTH), F3...  2.97 us

profile of v3, /device:TPU:1, one launch (start us, length us, event | category | flops | bytes accessed | tf_op | source)
XLA Modules:
  0.0 68.4 jit_solution(13321195116578194897)
XLA Ops:
  0.6 64.8 %range_finder.1 = (f32[2,2,4,256,128]{4,3,2,1,0:T(8,128)S(1)}, f32[256,256]{1,0:T(8,128)S(1)}, f32[256,256]{1,0:T(8,128)S(1)}) custom-call(f32[384,2048]{1,0:T(8,128)} %a_hbm.1, f32[2048,256]{1,0:T(8,128)} %t_hbm.1), custom_call_target="tpu_custom_call" | custom-call | tf_op jit(solution)/shard_map/range_finder/pallas_call | solution.py:425
  65.5 3.0 %final_product.1 = (f32[2048,256]{1,0:T(8,128)}, f32[256,256]{1,0:T(8,128)}) custom-call(f32[2,2048,128]{2,1,0:T(8,128)S(1)} %bitcast.1, f32[256,256]{1,0:T(8,128)S(1)} %get-tuple-element.6.w_ref, f32[256,256]{1,0:T(8,128)S(1)} %get-tuple-element.7.r_ref), custom_call_target="tpu_custom_call" | custom-call | tf_op jit(solution)/shard_map/final_product/pallas_call | solution.py:472

commit v4 on v3

--- a/solution.py
+++ b/solution.py
@@ -191,14 +191,19 @@
             x_gather(h, d).start()
 
     def cross(h, out_ref, core):
-        sketch = s_ref[h]
+        s1, s2, s3 = three_parts(s_ref[h])
+        near = jnp.concatenate([s1, s2], 1)
+        rest = jnp.concatenate([s3, s1], 0)
 
         @pl.loop(0, 4)
         def _(i):
             lines = pl.ds(pl.multiple_of(core * 1024 + i * 256, 256), 256)
-            out_ref[h, pl.ds(pl.multiple_of(i * 256, 256), 256), :] = jnp.dot(
-                at_ref[lines, :], sketch, precision=HIGH, preferred_element_type=F32
-            )
+            a1, a2, a3 = three_parts(at_ref[lines, :])
+            one = jnp.dot(a1, near, preferred_element_type=F32)
+            two = jnp.dot(a2, near, preferred_element_type=F32)
+            out = jnp.dot(jnp.concatenate([a1, a3], 1), rest, preferred_element_type=F32)
+            out = (out + two[:, HALF:]) + ((two[:, :HALF] + one[:, HALF:]) + one[:, :HALF])
+            out_ref[h, pl.ds(pl.multiple_of(i * 256, 256), 256), :] = out
 
     @tracked
     def s_scatter(h):
@@ -406,12 +411,16 @@
     triangle_ref[...] = r_ref[...] * (TOTAL**-0.5)
     copies = [pltpu.make_async_copy(triangle_ref, triangle_hbm, sem.at[4])]
     copies[0].start()
+    w1, w2, w3 = three_parts(w_ref[...])
+    low = jnp.concatenate([w3, w1, w2], 0)
     for i in range(4):
         lines = pl.ds(i * 512, 512)
-        out_ref[lines, :] = jnp.dot(
-            jnp.concatenate([z_ref[0, lines, :], z_ref[1, lines, :]], 1), w_ref[...],
-            precision=HIGH, preferred_element_type=F32,
-        )
+        z1, z2, z3 = three_parts(jnp.concatenate([z_ref[0, lines, :], z_ref[1, lines, :]], 1))
+        out_ref[lines, :] = (
+            jnp.dot(jnp.concatenate([z1, z3, z2], 1), low, preferred_element_type=F32)
+            + jnp.dot(z1, w2, preferred_element_type=F32)
+            + jnp.dot(z2, w1, preferred_element_type=F32)
+        ) + jnp.dot(z1, w1, preferred_element_type=F32)
         copies.append(pltpu.make_async_copy(out_ref.at[lines], out_hbm.at[lines], sem.at[i]))
         copies[-1].start()
     for copy in copies:

time: 68.5 us -> 68.5 us (level)
  no operation moved by 1% of the time
where the time goes in v4:
time: 68.5 us; the launch traced here: 68.4 us
  Pallas kernels  67.7 us (99%)
    pallas_call x1, Pallas kernels, body(): pl.pallas_call(kernel, out_shape=(jax.ShapeDtypeStruct((2, 2, NY, 256, HA...  64.9 us
    pallas_call x1, Pallas kernels, body(): pl.pallas_call(finish, out_shape=(jax.ShapeDtypeStruct((SNAPS, WIDTH), F3...  2.87 us

profile of v4, /device:TPU:1, one launch (start us, length us, event | category | flops | bytes accessed | tf_op | source)
XLA Modules:
  0.0 68.4 jit_solution(10983325363331744394)
XLA Ops:
  0.6 64.9 %range_finder.1 = (f32[2,2,4,256,128]{4,3,2,1,0:T(8,128)S(1)}, f32[256,256]{1,0:T(8,128)S(1)}, f32[256,256]{1,0:T(8,128)S(1)}) custom-call(f32[384,2048]{1,0:T(8,128)} %a_hbm.1, f32[2048,256]{1,0:T(8,128)} %t_hbm.1), custom_call_target="tpu_custom_call" | custom-call | tf_op jit(solution)/shard_map/range_finder/pallas_call | solution.py:434
  65.5 2.9 %final_product.1 = (f32[2048,256]{1,0:T(8,128)}, f32[256,256]{1,0:T(8,128)}) custom-call(f32[2,2048,128]{2,1,0:T(8,128)S(1)} %bitcast.1, f32[256,256]{1,0:T(8,128)S(1)} %get-tuple-element.6.w_ref, f32[256,256]{1,0:T(8,128)S(1)} %get-tuple-element.7.r_ref), custom_call_target="tpu_custom_call" | custom-call | tf_op jit(solution)/shard_map/final_product/pallas_call | solution.py:481
